TPU v7x, 32 devices: a whole 2x2x4 slice. The times are simulated.
32 devices in a mesh: dp: 8 (over y, x, core), mp: 4 (over z).
Axes of the slice: x: 2, y: 2, z: 4, core: 2. Of those that a mesh axis runs over, the one named last changes fastest.
Arguments:
- tokens: bfloat16 [12288, 1792], P(('dp', 'mp')), may hold values from -6 to 6
- cotangent: bfloat16 [12288, 1792], P(('dp', 'mp')), may hold values from -6 to 6
- route: int32 [12288], P(('dp', 'mp')), may hold values from 0 to 12287, as said below
- lengths: int32 [8, 3], P('dp'), may hold values from 1 to 1024, 1536 in all within a row
- key_mask: int32 [12288], P('dp'), may hold values 0 or 1
- norm1_gain: float32 [1792], replicated, may hold values from 0.1 to 1.9
- norm2_gain: float32 [1792], replicated, may hold values from 0.1 to 1.9
- w_query: bfloat16 [1792, 1792], P(None, 'mp'), may hold values from -0.1875 to 0.1875
- w_key: bfloat16 [1792, 1792], P(None, 'mp'), may hold values from -0.1875 to 0.1875
- w_value: bfloat16 [1792, 1792], P(None, 'mp'), may hold values from -0.125 to 0.125
- w_out: bfloat16 [1792, 1792], P('mp'), may hold values from -0.375 to 0.375
- w_gate: bfloat16 [1792, 4096], P(None, 'mp'), may hold values from -0.125 to 0.125
- w_up: bfloat16 [1792, 4096], P(None, 'mp'), may hold values from -0.125 to 0.125
- w_down: bfloat16 [4096, 1792], P('mp'), may hold values from -0.125 to 0.125
Outputs:
- output: bfloat16 [12288, 1792], P(('dp', 'mp'))
- input_grad: bfloat16 [12288, 1792], P(('dp', 'mp'))
- norm1_gain_grad: float32 [1792], replicated
- norm2_gain_grad: float32 [1792], replicated
- w_query_grad: float32 [1792, 1792], P(None, 'mp')
- w_key_grad: float32 [1792, 1792], P(None, 'mp')
- w_value_grad: float32 [1792, 1792], P(None, 'mp')
- w_out_grad: float32 [1792, 1792], P('mp')
- w_gate_grad: float32 [1792, 4096], P(None, 'mp')
- w_up_grad: float32 [1792, 4096], P(None, 'mp')
- w_down_grad: float32 [4096, 1792], P('mp')
Inputs may be any that keep to these rules, and one draw needn't show every extreme that they name: route is a permutation of the 12288 slots. For every row r, slot s = route[r] lies on index s // 1536 of dp and on index (s // 384) % (number of mp indices) of mp, and that mp index equals the mp index of the device that holds row r in given order; every device holds exactly 48 rows bound for each index of dp. Each row of lengths sums to 1536; its largest entry is exactly 1024.
All inputs are finite; a program needn't handle non-finite values. No bound on the sum of `key_mask` on one device may be relied on, other than what follows from the above.
Results may differ from a plain program's by a relative error of at most 0.019.
Values may be sent and summed in bfloat16 or wider, within the bound.
A program may use at most 192 MiB of HBM per device.

v0:
```python
import jax
import jax.numpy as jnp
from jax import lax
from jax.sharding import PartitionSpec as P

HEAD_DIM = 112
WINDOW = 64
TOK_DEV = 1536
EPSILON = 1e-05
MASKED = 1e30


def norm_rows(values):
    inverse = lax.rsqrt(jnp.mean(values * values, axis=-1, keepdims=True) + EPSILON)
    return (values * inverse, inverse)


def norm_back(gradient, normed, inverse, norm_gain):
    scaled = gradient * norm_gain
    result = inverse * (scaled - normed * jnp.mean(scaled * normed, axis=-1, keepdims=True))
    return (result, jnp.sum(gradient * normed, axis=0))


def padded(values, filler):
    front = jnp.full((WINDOW,) + values.shape[1:], filler, values.dtype)
    return jnp.concatenate([front, values], axis=0)


def block_scores(query_block, key_block, query_seg, key_seg, key_flag, first_row, score_scale):
    query_pos = first_row + jnp.arange(query_block.shape[0], dtype=jnp.int32)
    key_pos = first_row - WINDOW + jnp.arange(key_block.shape[0], dtype=jnp.int32)
    distance = query_pos[:, None] - key_pos[None, :]
    allowed = (distance >= 0) & (distance < WINDOW) & (query_seg[:, None] == key_seg[None, :])
    allowed = allowed & ((key_flag[None, :] == 1) | (distance == 0))
    raw_scores = (
        jnp.einsum("qhd,khd->hqk", query_block, key_block, preferred_element_type=jnp.float32)
        * score_scale
    )
    return jnp.where(allowed[None], raw_scores, -MASKED)


def block_inputs(query, key_pad, value_pad, segment, seg_pad, live_pad, first_row, block_rows):
    key_span = block_rows + WINDOW
    return (
        lax.dynamic_slice_in_dim(query, first_row, block_rows, 0),
        lax.dynamic_slice_in_dim(key_pad, first_row, key_span, 0),
        lax.dynamic_slice_in_dim(value_pad, first_row, key_span, 0),
        lax.dynamic_slice_in_dim(segment, first_row, block_rows, 0),
        lax.dynamic_slice_in_dim(seg_pad, first_row, key_span, 0),
        lax.dynamic_slice_in_dim(live_pad, first_row, key_span, 0),
    )


def attend_forward(query, key_all, value_all, segment, key_live):
    token_count, head_count, head_width = query.shape
    block_rows = min(512, token_count)
    score_scale = head_width ** (-0.5)
    key_pad = padded(key_all, 0.0)
    value_pad = padded(value_all, 0.0)
    seg_pad = padded(segment, -1)
    live_pad = padded(key_live, 0)

    def one_block(running, block_index):
        first_row = block_index * block_rows
        query_block, key_block, value_block, query_seg, key_seg, key_flag = block_inputs(
            query, key_pad, value_pad, segment, seg_pad, live_pad, first_row, block_rows
        )
        scores = block_scores(
            query_block, key_block, query_seg, key_seg, key_flag, first_row, score_scale
        )
        row_max = jnp.max(scores, axis=-1, keepdims=True)
        weights = jnp.exp(scores - row_max)
        denominator = jnp.sum(weights, axis=-1, keepdims=True)
        chances = (weights / denominator).astype(jnp.bfloat16)
        mixed = jnp.einsum("hqk,khd->qhd", chances, value_block, preferred_element_type=jnp.float32)
        return (
            running,
            (mixed.astype(jnp.bfloat16), row_max[..., 0] + jnp.log(denominator[..., 0])),
        )

    _, (mixed, logsum) = lax.scan(
        one_block, jnp.zeros((), jnp.int32), jnp.arange(token_count // block_rows, dtype=jnp.int32)
    )
    return (mixed.reshape(token_count, head_count * head_width), logsum)


def attend_backward(query, key_all, value_all, segment, key_live, logsum, mixed_grad):
    token_count, head_count, head_width = query.shape
    block_rows = min(512, token_count)
    key_span = block_rows + WINDOW
    score_scale = head_width ** (-0.5)
    key_pad = padded(key_all, 0.0)
    value_pad = padded(value_all, 0.0)
    seg_pad = padded(segment, -1)
    live_pad = padded(key_live, 0)

    def one_block(running, inputs):
        key_grad, value_grad = running
        block_index, block_logsum = inputs
        first_row = block_index * block_rows
        query_block, key_block, value_block, query_seg, key_seg, key_flag = block_inputs(
            query, key_pad, value_pad, segment, seg_pad, live_pad, first_row, block_rows
        )
        grad_block = lax.dynamic_slice_in_dim(mixed_grad, first_row, block_rows, 0)
        scores = block_scores(
            query_block, key_block, query_seg, key_seg, key_flag, first_row, score_scale
        )
        chances = jnp.exp(scores - block_logsum[..., None])
        chance_grad = jnp.einsum(
            "qhd,khd->hqk", grad_block, value_block, preferred_element_type=jnp.float32
        )
        row_dot = jnp.sum(chances * chance_grad, axis=-1, keepdims=True)
        score_grad = (chances * (chance_grad - row_dot)).astype(jnp.bfloat16)
        query_grad = (
            jnp.einsum("hqk,khd->qhd", score_grad, key_block, preferred_element_type=jnp.float32)
            * score_scale
        )
        key_part = (
            jnp.einsum("hqk,qhd->khd", score_grad, query_block, preferred_element_type=jnp.float32)
            * score_scale
        )
        value_part = jnp.einsum(
            "hqk,qhd->khd",
            chances.astype(jnp.bfloat16),
            grad_block,
            preferred_element_type=jnp.float32,
        )
        key_grad = lax.dynamic_update_slice_in_dim(
            key_grad,
            lax.dynamic_slice_in_dim(key_grad, first_row, key_span, 0) + key_part,
            first_row,
            0,
        )
        value_grad = lax.dynamic_update_slice_in_dim(
            value_grad,
            lax.dynamic_slice_in_dim(value_grad, first_row, key_span, 0) + value_part,
            first_row,
            0,
        )
        return ((key_grad, value_grad), query_grad)

    empty_grad = jnp.zeros((token_count + WINDOW, head_count, head_width), jnp.float32)
    (key_grad, value_grad), query_grad = lax.scan(
        one_block,
        (empty_grad, empty_grad),
        (jnp.arange(token_count // block_rows, dtype=jnp.int32), logsum),
    )
    flat_width = head_count * head_width
    return (
        query_grad.reshape(token_count, flat_width).astype(jnp.bfloat16),
        key_grad[WINDOW:].reshape(token_count, flat_width).astype(jnp.bfloat16),
        value_grad[WINDOW:].reshape(token_count, flat_width).astype(jnp.bfloat16),
    )


def local(
    tokens,
    cotangent,
    route,
    lengths,
    key_mask,
    norm1_gain,
    norm2_gain,
    w_query,
    w_key,
    w_value,
    w_out,
    w_gate,
    w_up,
    w_down,
):
    groups = lax.axis_size("dp")
    members = lax.axis_size("mp")
    member = lax.axis_index("mp")
    local_rows = tokens.shape[0]
    group_rows = local_rows * members
    bucket = local_rows // groups
    target = route // TOK_DEV
    chosen = (target[:, None] == jnp.arange(groups, dtype=jnp.int32)[None, :]).astype(jnp.int32)
    ranking = jnp.sum((jnp.cumsum(chosen, axis=0) - chosen) * chosen, axis=1)
    send_at = target * bucket + ranking
    arrival, arrival_grad, arrival_slot = (
        lax.all_to_all(
            jnp.zeros_like(tokens).at[send_at].set(tokens),
            "dp",
            split_axis=0,
            concat_axis=0,
            tiled=True,
        ),
        lax.all_to_all(
            jnp.zeros_like(cotangent).at[send_at].set(cotangent),
            "dp",
            split_axis=0,
            concat_axis=0,
            tiled=True,
        ),
        lax.all_to_all(
            jnp.zeros_like(route).at[send_at].set(route % local_rows),
            "dp",
            split_axis=0,
            concat_axis=0,
            tiled=True,
        ),
    )
    token_rows = jnp.zeros_like(arrival).at[arrival_slot].set(arrival)
    grad_rows = jnp.zeros_like(arrival_grad).at[arrival_slot].set(arrival_grad)
    seq_ends = jnp.cumsum(lengths[0])
    positions = jnp.arange(group_rows, dtype=jnp.int32)
    segment = jnp.sum((positions[:, None] >= seq_ends[None, :]).astype(jnp.int32), axis=1)
    input_rows = token_rows.astype(jnp.float32)
    normed_one, inverse_one = norm_rows(input_rows)
    leading_all, grad_all = (
        lax.all_gather(token_rows, "mp", axis=0, tiled=True),
        lax.all_gather(grad_rows, "mp", axis=0, tiled=True),
    )
    input_all = leading_all.astype(jnp.float32)
    normed_all, _ = norm_rows(input_all)
    hidden_one = (normed_all * norm1_gain).astype(jnp.bfloat16)
    head_count = w_query.shape[1] // HEAD_DIM
    query = jnp.dot(hidden_one, w_query, preferred_element_type=jnp.float32).astype(jnp.bfloat16)
    keys = jnp.dot(hidden_one, w_key, preferred_element_type=jnp.float32).astype(jnp.bfloat16)
    values = jnp.dot(hidden_one, w_value, preferred_element_type=jnp.float32).astype(jnp.bfloat16)
    query_heads = query.reshape(group_rows, head_count, HEAD_DIM)
    key_heads = keys.reshape(group_rows, head_count, HEAD_DIM)
    value_heads = values.reshape(group_rows, head_count, HEAD_DIM)
    mixed_flat, logsum = attend_forward(query_heads, key_heads, value_heads, segment, key_mask)
    attention_all = lax.psum(jnp.dot(mixed_flat, w_out, preferred_element_type=jnp.float32), "mp")
    middle_all = input_all + attention_all
    middle_rows = lax.dynamic_slice_in_dim(middle_all, member * local_rows, local_rows, 0)
    normed_mid, _ = norm_rows(middle_all)
    hidden_two = (normed_mid * norm2_gain).astype(jnp.bfloat16)
    normed_two, inverse_two = norm_rows(middle_rows)
    gate_value = jnp.dot(hidden_two, w_gate, preferred_element_type=jnp.float32)
    upward = jnp.dot(hidden_two, w_up, preferred_element_type=jnp.float32)
    sigmoid = jax.nn.sigmoid(gate_value)
    activated = (gate_value * sigmoid * upward).astype(jnp.bfloat16)
    out_rows = middle_rows + lax.psum_scatter(
        jnp.dot(activated, w_down, preferred_element_type=jnp.float32).astype(jnp.bfloat16),
        "mp",
        scatter_dimension=0,
        tiled=True,
    ).astype(jnp.float32)
    activated_grad = jnp.einsum("td,fd->tf", grad_all, w_down, preferred_element_type=jnp.float32)
    gate_grad = (activated_grad * upward * sigmoid * (1.0 + gate_value * (1.0 - sigmoid))).astype(
        jnp.bfloat16
    )
    upward_grad = (activated_grad * gate_value * sigmoid).astype(jnp.bfloat16)
    down_sum = jnp.einsum("tf,td->fd", activated, grad_all, preferred_element_type=jnp.float32)
    gate_sum = jnp.einsum("td,tf->df", hidden_two, gate_grad, preferred_element_type=jnp.float32)
    upward_sum = jnp.einsum(
        "td,tf->df", hidden_two, upward_grad, preferred_element_type=jnp.float32
    )
    hidden_two_grad = lax.psum_scatter(
        jnp.einsum("tf,df->td", gate_grad, w_gate, preferred_element_type=jnp.float32)
        + jnp.einsum("tf,df->td", upward_grad, w_up, preferred_element_type=jnp.float32),
        "mp",
        scatter_dimension=0,
        tiled=True,
    )
    norm_part_two, gain_two_grad = norm_back(hidden_two_grad, normed_two, inverse_two, norm2_gain)
    middle_grad = grad_rows.astype(jnp.float32) + norm_part_two
    branch_all = lax.all_gather(middle_grad.astype(jnp.bfloat16), "mp", axis=0, tiled=True)
    output_sum = jnp.einsum("tc,td->cd", mixed_flat, branch_all, preferred_element_type=jnp.float32)
    mixed_grad = jnp.einsum(
        "td,cd->tc", branch_all, w_out, preferred_element_type=jnp.float32
    ).astype(jnp.bfloat16)
    query_grad, key_grad, value_grad = attend_backward(
        query_heads,
        key_heads,
        value_heads,
        segment,
        key_mask,
        logsum,
        mixed_grad.reshape(group_rows, head_count, HEAD_DIM),
    )
    query_sum = jnp.einsum("td,tc->dc", hidden_one, query_grad, preferred_element_type=jnp.float32)
    key_sum = jnp.einsum("td,tc->dc", hidden_one, key_grad, preferred_element_type=jnp.float32)
    value_sum = jnp.einsum("td,tc->dc", hidden_one, value_grad, preferred_element_type=jnp.float32)
    hidden_one_grad = lax.psum_scatter(
        (
            jnp.einsum("tc,dc->td", query_grad, w_query, preferred_element_type=jnp.float32)
            + jnp.einsum("tc,dc->td", key_grad, w_key, preferred_element_type=jnp.float32)
            + jnp.einsum("tc,dc->td", value_grad, w_value, preferred_element_type=jnp.float32)
        ).astype(jnp.bfloat16),
        "mp",
        scatter_dimension=0,
        tiled=True,
    ).astype(jnp.float32)
    norm_part_one, gain_one_grad = norm_back(hidden_one_grad, normed_one, inverse_one, norm1_gain)
    input_grad = middle_grad + norm_part_one
    gain_one_sum, gain_two_sum = lax.psum((gain_one_grad, gain_two_grad), ("dp", "mp"))
    weight_sums = (
        lax.psum(query_sum.astype(jnp.bfloat16), "dp").astype(jnp.float32),
        lax.psum(key_sum.astype(jnp.bfloat16), "dp").astype(jnp.float32),
        lax.psum(value_sum.astype(jnp.bfloat16), "dp").astype(jnp.float32),
        lax.psum(output_sum.astype(jnp.bfloat16), "dp").astype(jnp.float32),
        lax.psum(gate_sum.astype(jnp.bfloat16), "dp").astype(jnp.float32),
        lax.psum(upward_sum.astype(jnp.bfloat16), "dp").astype(jnp.float32),
        lax.psum(down_sum.astype(jnp.bfloat16), "dp").astype(jnp.float32),
    )
    back_out, back_grad = (
        lax.all_to_all(
            out_rows.astype(jnp.bfloat16)[arrival_slot],
            "dp",
            split_axis=0,
            concat_axis=0,
            tiled=True,
        ),
        lax.all_to_all(
            input_grad.astype(jnp.bfloat16)[arrival_slot],
            "dp",
            split_axis=0,
            concat_axis=0,
            tiled=True,
        ),
    )
    return (
        back_out[send_at],
        back_grad[send_at],
        gain_one_sum,
        gain_two_sum,
        weight_sums[0],
        weight_sums[1],
        weight_sums[2],
        weight_sums[3],
        weight_sums[4],
        weight_sums[5],
        weight_sums[6],
    )


def solution(mesh):
    in_specs = (
        P(("dp", "mp"), None),
        P(("dp", "mp"), None),
        P(("dp", "mp")),
        P("dp", None),
        P("dp"),
        P(),
        P(),
        P(None, "mp"),
        P(None, "mp"),
        P(None, "mp"),
        P("mp", None),
        P(None, "mp"),
        P(None, "mp"),
        P("mp", None),
    )
    out_specs = (
        P(("dp", "mp"), None),
        P(("dp", "mp"), None),
        P(),
        P(),
        P(None, "mp"),
        P(None, "mp"),
        P(None, "mp"),
        P("mp", None),
        P(None, "mp"),
        P(None, "mp"),
        P("mp", None),
    )
    return jax.shard_map(local, mesh=mesh, in_specs=in_specs, out_specs=out_specs, check_vma=False)
```

profile of v0, /device:TPU:0, one launch (start us, length us, event | category | flops | bytes accessed | tf_op | source)
XLA Modules:
  0.0 1727.3 jit_solution(16116755077285871703)
XLA Ops:
  28.3 17.6 %all-to-all-done.1 = bf16[8,48,1792]{2,1,0:T(8,128)(2,1)S(1)} async-done(((bf16[8,48,1792]{2,1,0:T(8,128)(2,1)}), bf16[8,48,1792]{2,1,0:T(8,128)(2,1)S(1)}, u32[]{:S(2)}, u32[]{:S(2)}) %all-to-all-start.1) | async-done | bytes 1376288 | tf_op jit(solution)/shard_map/all_to_all | solution.py:183
  50.2 101.4 %all-gather.4.cloned.1.call-done = bf16[1536,1792]{1,0:T(8,128)(2,1)} async-done(((bf16[384,1792]{1,0:T(8,128)(2,1)}), bf16[1536,1792]{1,0:T(8,128)(2,1)}) %all-gather.4.cloned.1.call-update) | async-done | bytes 5505040 | tf_op jit(solution)/shard_map/all_gather | solution.py:213
  169.8 26.9 %while.30 = (s32[]{:T(128)}, bf16[3,512,4,112]{1,3,2,0:T(8,128)(2,1)}, f32[3,4,512]{2,1,0:T(4,128)S(1)}, s32[3]{0:T(128)S(1)}, bf16[1600,4,112]{0,2,1:T(8,128)(2...) while((s32[]{:T(128)}, ...), condition=%wide.region_12.13_spmd, body=%wide.region_9.12_spmd.sunk | while | flops 545521280 | bytes 17490852 | solution.py:81
  204.2 7.9 fusion.83
  216.8 23.1 %all_to_all.60 = bf16[8,48,1792]{2,1,0:T(8,128)(2,1)} all-to-all(bf16[8,48,1792]{2,1,0:T(8,128)(2,1)} %bitcast.130), channel_id=1, replica_groups=mesh['dp'=8,'mp'=4] {'dp'}, dimensions={0} | all-to-all | bytes 2752512 | tf_op jit(solution)/shard_map/all_to_all | solution.py:190
  244.6 341.4 %all-reduce.9.cloned.1.call-done = f32[1536,1792]{1,0:T(8,128)} async-done(((f32[1536,1792]{1,0:T(8,128)}), f32[1536,1792]{1,0:T(8,128)}) %all-reduce.9.cloned.1.call-update) | async-done | bytes 11010064 | tf_op jit(solution)/shard_map/psum | solution.py:227
  586.1 11.9 multiply_reduce_fusion.1
  603.1 11.5 fusion.84
  614.6 7.7 fusion.85
  622.3 66.7 %all-gather.6.cloned.1.call-done = bf16[1536,1792]{1,0:T(8,128)(2,1)} async-done(((bf16[384,1792]{1,0:T(8,128)(2,1)}), bf16[1536,1792]{1,0:T(8,128)(2,1)}) %all-gather.6.cloned.1.call-update) | async-done | bytes 5505040 | tf_op jit(solution)/shard_map/all_gather | solution.py:214
  689.0 16.0 multiply_convert_fusion.2
  705.1 8.5 fusion.86
  713.6 11.2 convolution_add_fusion
  726.9 182.8 %reduce-scatter.6.cloned.1.call-done = f32[384,1792]{1,0:T(8,128)} async-done(((f32[1536,1792]{1,0:T(8,128)}), f32[384,1792]{1,0:T(8,128)}) %reduce-scatter.6.cloned.1.call-update) | async-done | bytes 2752528 | tf_op jit(solution)/shard_map/reduce_scatter | solution.py:253
  918.2 103.5 %all-gather.8.cloned.1.call-done = bf16[1536,1792]{1,0:T(8,128)(2,1)} async-done(((bf16[384,1792]{1,0:T(8,128)(2,1)}), bf16[1536,1792]{1,0:T(8,128)(2,1)}) %all-gather.8.cloned.1.call-update) | async-done | bytes 5505040 | tf_op jit(solution)/shard_map/all_gather | solution.py:262
  1032.5 127.1 %while.31 = (s32[]{:T(128)}, f32[1600,4,112]{0,2,1:T(8,128)}, f32[1600,4,112]{0,2,1:T(8,128)}, bf16[3,512,4,112]{1,3,2,0:T(8,128)(2,1)}, s32[3]{0:T(128)S(1)}, /...) while((s32[]{:T(128)}, f32[1600,4,112]{0,2,1:T(8,128)}, ...), condition=%wide.region_24.25_spmd, body=%wide.region_22.24_spmd.sunk | while | flops 1342557824 | bytes 73204776 | solution.py:143
  1049.1 9.8 dynamic_update_slice.44
  1063.3 9.8 dynamic_update_slice.45
  1092.8 9.7 dynamic_update_slice.44
  1106.8 9.7 dynamic_update_slice.45
  1136.0 8.1 dynamic_update_slice.44
  1148.5 8.1 dynamic_update_slice.45
  1180.5 7.5 add_convert_fusion
  1188.0 10.1 convolution_convert_fusion
  1198.2 10.7 convolution_convert_fusion.1
  1209.0 10.3 convolution_convert_fusion.3
  1219.3 7.4 convolution_convert_fusion.2
  1243.9 40.6 %reduce-scatter.8.cloned.1.call-done = bf16[384,1792]{1,0:T(8,128)(2,1)} async-done(((bf16[1536,1792]{1,0:T(8,128)(2,1)}), bf16[384,1792]{1,0:T(8,128)(2,1)}) %reduce-scatter.8.cloned.1.call-update) | async-done | bytes 1376272 | tf_op jit(solution)/shard_map/reduce_scatter | solution.py:279
  1286.8 99.1 %reduce-scatter.4.cloned.1.call-done = bf16[384,1792]{1,0:T(8,128)(2,1)} async-done(((bf16[1536,1792]{1,0:T(8,128)(2,1)}), bf16[384,1792]{1,0:T(8,128)(2,1)}) %reduce-scatter.4.cloned.1.call-update) | async-done | bytes 1376272 | tf_op jit(solution)/shard_map/reduce_scatter | solution.py:237
  1400.7 30.8 %all-to-all-done.2 = bf16[8,48,1792]{2,1,0:T(8,128)(2,1)S(1)} async-done(((bf16[8,48,1792]{2,1,0:T(8,128)(2,1)}), bf16[8,48,1792]{2,1,0:T(8,128)(2,1)S(1)}, u32[]{:S(2)}, u32[]{:S(2)}) %all-to-all-start.2) | async-done | bytes 1376288 | tf_op jit(solution)/shard_map/all_to_all | solution.py:302
  1436.1 213.3 %all-reduce.11.cloned.1.call-done = (bf16[1792,448]{0,1:T(8,128)(2,1)}, bf16[1792,448]{0,1:T(8,128)(2,1)}, bf16[1792,448]{0,1:T(8,128)(2,1)}, bf16[448,1792]{1,0...) async-done(((bf16[1792,448]{0,1:T(8,128)(2,1)}, bf16[1792,448]{0,1:T(8,128)(2,1)}, bf16[1792,448]{0,1:T(8,128)(2,1)}, ...) | async-done | bytes 17432592 | tf_op jit(solution)/shard_map/psum | solution.py:293
  1671.4 39.4 %all-reduce.4 = (f32[1792]{0:T(1024)}, f32[1792]{0:T(1024)}) all-reduce(f32[1792]{0:T(1024)S(1)} %get-tuple-element.307, f32[1792]{0:T(1024)S(1)} %copy-done.27), channel_id=1, replica_groups=mesh['dp'=8,'mp'=4] {'dp','mp'}, use_global_device_ids=true, to_apply=%region_28.29 | all-reduce | flops 3584 | bytes 28672 | tf_op jit(solution)/shard_map/psum | solution.py:291
  (297 shorter events, 272.0 us)
Async XLA Ops:
  7.2 197.1 %copy-start = (bf16[448,1792]{1,0:T(8,128)(2,1)S(1)}, bf16[448,1792]{1,0:T(8,128)(2,1)}, u32[]{:S(2)}) copy-start(bf16[448,1792]{1,0:T(8,128)(2,1)} %param.28) | copy-start | bytes 4816900
  9.3 203.0 %copy-start.30 = (s32[384]{0:T(512)}, s32[384]{0:T(512)S(1)}, u32[]{:S(2)}) copy-start(s32[384]{0:T(512)S(1)} %compare_select_fusion.1) | copy-start | bytes 4612
  12.9 9.8 all-to-all-start
  22.6 27.1 %copy-start.41 = (s32[1,3]{1,0:T(1,128)S(1)}, s32[1,3]{1,0:T(1,128)}, u32[]{:S(2)}) copy-start(s32[1,3]{1,0:T(1,128)} %param.21) | copy-start | bytes 40
  22.6 27.3 %copy-start.34 = (s32[1536]{0:T(1024)S(1)}, s32[1536]{0:T(1024)}, u32[]{:S(2)}) copy-start(s32[1536]{0:T(1024)} %param.22) | copy-start | bytes 18436
  22.6 23.2 %all-to-all-start.1 = ((bf16[8,48,1792]{2,1,0:T(8,128)(2,1)}), bf16[8,48,1792]{2,1,0:T(8,128)(2,1)S(1)}, u32[]{:S(2)}, u32[]{:S(2)}) async-start(bf16[8,48,1792]{2,1,0:T(8,128)(2,1)} %bitcast.14), calls=%async_computation.1 | async-start | bytes 2752512 | tf_op jit(solution)/shard_map/all_to_all | solution.py:183
  26.9 124.7 %all-gather.4.cloned.1.call-start = ((), (), s32[]{:S(2)}) async-start(), calls=%async_computation.8 | async-start | bytes 6881280 | tf_op jit(solution)/shard_map/all_gather | solution.py:213
  28.3 211.7 %copy-start.32 = (s32[384]{0:T(512)}, s32[384]{0:T(512)S(1)}, u32[]{:S(2)}) copy-start(s32[384]{0:T(512)S(1)} %fusion.79) | copy-start | bytes 4612
  49.7 536.4 %all-reduce.9.cloned.1.call-start = ((), (), s32[]{:S(2)}) async-start(), calls=%async_computation.9 | async-start | bytes 22020096 | tf_op jit(solution)/shard_map/psum | solution.py:227
  50.2 105.3 %copy-start.23 = (f32[1792]{0:T(1024)S(1)}, f32[1792]{0:T(1024)}, u32[]{:S(2)}) copy-start(f32[1792]{0:T(1024)} %param.23) | copy-start | bytes 21508
  212.2 476.8 %all-gather.6.cloned.1.call-start = ((), (), s32[]{:S(2)}) async-start(), calls=%async_computation.11 | async-start | bytes 6881280 | tf_op jit(solution)/shard_map/all_gather | solution.py:214
  244.6 353.4 %copy-start.21 = (f32[1792]{0:T(1024)S(1)}, f32[1792]{0:T(1024)}, u32[]{:S(2)}) copy-start(f32[1792]{0:T(1024)} %param.24) | copy-start | bytes 21508
  244.6 665.2 %reduce-scatter.6.cloned.1.call-start = ((), (), s32[]{:S(2)}) async-start(), calls=%async_computation.12 | async-start | bytes 13762560 | tf_op jit(solution)/shard_map/reduce_scatter | solution.py:253
  603.1 11.6 copy-start.7
  603.1 11.6 copy-start.36
  689.0 16.0 copy-start.35
  724.8 297.0 %all-gather.8.cloned.1.call-start = ((), (), s32[]{:S(2)}) async-start(), calls=%async_computation.13 | async-start | bytes 6881280 | tf_op jit(solution)/shard_map/all_gather | solution.py:262
  726.9 186.9 %copy-start.25 = (f32[384]{0:T(512)}, f32[384]{0:T(512)S(1)}, u32[]{:S(2)}) copy-start(f32[384]{0:T(512)S(1)} %add_rsqrt_fusion.3) | copy-start | bytes 4612
  918.2 366.3 %reduce-scatter.8.cloned.1.call-start = ((), (), s32[]{:S(2)}) async-start(), calls=%async_computation.14 | async-start | bytes 6881280 | tf_op jit(solution)/shard_map/reduce_scatter | solution.py:279
  1188.0 197.9 %reduce-scatter.4.cloned.1.call-start = ((), (), s32[]{:S(2)}) async-start(), calls=%async_computation.10 | async-start | bytes 6881280 | tf_op jit(solution)/shard_map/reduce_scatter | solution.py:237
  1198.1 451.2 %all-reduce.11.cloned.1.call-start = ((), (), s32[]{:S(2)}) async-start(), calls=%async_computation.15 | async-start | bytes 34865152 | tf_op jit(solution)/shard_map/psum | solution.py:293
  1198.2 10.8 copy-start.45
  1198.2 21.1 %slice-start.2 = ((s8[5505024]{0:T(1024)(128)(4,1)}), s8[4194304]{0:T(1024)(128)(4,1)S(1)}, s32[]{:S(2)}) async-start(s8[5505024]{0:T(1024)(128)(4,1)} %bitcast.124), calls=%async_computation.18 | async-start | bytes 8388608
  1208.9 17.8 %slice-start.4 = ((s8[5505024]{0:T(1024)(128)(4,1)}), s8[4194304]{0:T(1024)(128)(4,1)S(1)}, s32[]{:S(2)}) async-start(s8[5505024]{0:T(1024)(128)(4,1)} %bitcast.128), calls=%async_computation.20 | async-start | bytes 8388608
  1226.7 11.6 slice-start.6
  1242.2 42.3 %copy-start.24 = (f32[1792]{0:T(1024)S(1)}, f32[1792]{0:T(1024)}, u32[]{:S(2)}) copy-start(f32[1792]{0:T(1024)} %param.23) | copy-start | bytes 21508
  1242.8 143.1 %copy-start.22 = (f32[1792]{0:T(1024)S(1)}, f32[1792]{0:T(1024)}, u32[]{:S(2)}) copy-start(f32[1792]{0:T(1024)} %param.24) | copy-start | bytes 21508
  1242.8 143.1 %copy-start.26 = (f32[384]{0:T(512)S(1)}, f32[384]{0:T(512)}, u32[]{:S(2)}) copy-start(f32[384]{0:T(512)} %copy-done.25) | copy-start | bytes 4612
  1242.8 143.1 %copy-start.29 = (f32[384]{0:T(512)S(1)}, f32[384]{0:T(512)}, u32[]{:S(2)}) copy-start(f32[384]{0:T(512)} %copy-done.28) | copy-start | bytes 4612
  1394.1 37.5 %all-to-all-start.2 = ((bf16[8,48,1792]{2,1,0:T(8,128)(2,1)}), bf16[8,48,1792]{2,1,0:T(8,128)(2,1)S(1)}, u32[]{:S(2)}, u32[]{:S(2)}) async-start(bf16[8,48,1792]{2,1,0:T(8,128)(2,1)} %bitcast.127), calls=%async_computation.3 | async-start | bytes 2752512 | tf_op jit(solution)/shard_map/all_to_all | solution.py:302
  1400.7 35.4 %copy-start.31 = (s32[384]{0:T(512)S(1)}, s32[384]{0:T(512)}, u32[]{:S(2)}) copy-start(s32[384]{0:T(512)} %copy-done.30) | copy-start | bytes 4612
  1431.5 282.3 %all-to-all-start.4 = ((bf16[8,48,1792]{2,1,0:T(8,128)(2,1)}), bf16[8,48,1792]{2,1,0:T(8,128)(2,1)}, u32[]{:S(2)}, u32[]{:S(2)}) async-start(bf16[8,48,1792]{2,1,0:T(8,128)(2,1)} %bitcast.126), calls=%async_computation.7 | async-start | bytes 2752512 | tf_op jit(solution)/shard_map/all_to_all | solution.py:309
  (40 other events, 178.6 us)
Sparse Core Ops, SparseCore 0:
  49.8 101.7 all-gather.3
  212.3 373.7 all-reduce.8
  587.6 101.3 all-gather.5
  724.9 184.7 reduce-scatter.5
  918.3 103.4 all-gather.7
  1188.1 96.3 reduce-scatter.7
  1287.3 98.5 reduce-scatter.3
  1391.7 257.6 all-reduce.10
where the time goes:
time: 1740 us; the launch traced here: 1730 us
  waiting for transfers between devices  1200 us (69%)
  matrix products  226 us (13%)
  local copies, waits for them, and re-layouts  130 us (7%)
  other arithmetic  74.3 us (4%)
  blocking collectives  62.6 us (4%)
  starting transfers between devices  18 us (1%)
    psum x1, waiting for transfers between devices, local(): lax.psum(jnp.dot(mixed_flat, w_out, preferred_element_type=jnp.float32),...  341 us
    psum x1, waiting for transfers between devices, local(): lax.psum(query_sum.astype(jnp.bfloat16), 'dp').astype(jnp.float32)  213 us
    reduce_scatter x1, waiting for transfers between devices, local(): lax.psum_scatter(jnp.einsum('tf,df->td', gate_grad, w_gate, preferred_ele...  183 us
    all_gather x1, waiting for transfers between devices, local(): lax.all_gather(middle_grad.astype(jnp.bfloat16), 'mp', axis=0, tiled=True)  104 us
    all_gather x1, waiting for transfers between devices, local(): lax.all_gather(token_rows, 'mp', axis=0, tiled=True)  101 us
    reduce_scatter x1, waiting for transfers between devices, local(): lax.psum_scatter(jnp.dot(activated, w_down, preferred_element_type=jnp.fl...  99.1 us
    all_gather x1, waiting for transfers between devices, local(): lax.all_gather(grad_rows, 'mp', axis=0, tiled=True)  66.7 us
    reduce_scatter x1, waiting for transfers between devices, local(): lax.psum_scatter((jnp.einsum('tc,dc->td', query_grad, w_query, preferred_...  40.6 us
  transfers between devices with their start and end apart: 12, of which 10 were waited for; matrix products, arithmetic and copies ran while one was open for 8% of the time, Pallas kernels for 0%

commit v1 on v0

--- a/solution.py
+++ b/solution.py
@@ -288,7 +288,7 @@
     ).astype(jnp.float32)
     norm_part_one, gain_one_grad = norm_back(hidden_one_grad, normed_one, inverse_one, norm1_gain)
     input_grad = middle_grad + norm_part_one
-    gain_one_sum, gain_two_sum = lax.psum((gain_one_grad, gain_two_grad), ("dp", "mp"))
+    gain_one_sum, gain_two_sum = lax.psum(lax.psum((gain_one_grad, gain_two_grad), "dp"), "mp")
     weight_sums = (
         lax.psum(query_sum.astype(jnp.bfloat16), "dp").astype(jnp.float32),
         lax.psum(key_sum.astype(jnp.bfloat16), "dp").astype(jnp.float32),

time: 1740 us -> 1740 us (level)
    psum x1 -> x2, blocking collectives: 39.4 us -> 42.5 us  [the longest x1 23.2 us: local(): lax.psum((gain_one_grad, gain_two_grad), 'dp')]
where the time goes in v1:
time: 1740 us; the launch traced here: 1730 us
  waiting for transfers between devices  1200 us (69%)
  matrix products  226 us (13%)
  local copies, waits for them, and re-layouts  129 us (7%)
  other arithmetic  74.3 us (4%)
  blocking collectives  65.7 us (4%)
  starting transfers between devices  18 us (1%)
    psum x1, waiting for transfers between devices, local(): lax.psum(jnp.dot(mixed_flat, w_out, preferred_element_type=jnp.float32),...  341 us
    psum x1, waiting for transfers between devices, local(): lax.psum(query_sum.astype(jnp.bfloat16), 'dp').astype(jnp.float32)  213 us
    reduce_scatter x1, waiting for transfers between devices, local(): lax.psum_scatter(jnp.einsum('tf,df->td', gate_grad, w_gate, preferred_ele...  183 us
    all_gather x1, waiting for transfers between devices, local(): lax.all_gather(middle_grad.astype(jnp.bfloat16), 'mp', axis=0, tiled=True)  104 us
    all_gather x1, waiting for transfers between devices, local(): lax.all_gather(token_rows, 'mp', axis=0, tiled=True)  101 us
    reduce_scatter x1, waiting for transfers between devices, local(): lax.psum_scatter(jnp.dot(activated, w_down, preferred_element_type=jnp.fl...  99.1 us
    all_gather x1, waiting for transfers between devices, local(): lax.all_gather(grad_rows, 'mp', axis=0, tiled=True)  66.7 us
    reduce_scatter x1, waiting for transfers between devices, local(): lax.psum_scatter((jnp.einsum('tc,dc->td', query_grad, w_query, preferred_...  40.6 us
  transfers between devices with their start and end apart: 12, of which 10 were waited for; matrix products, arithmetic and copies ran while one was open for 8% of the time, Pallas kernels for 0%

profile of v1, /device:TPU:0, one launch (start us, length us, event | category | flops | bytes accessed | tf_op | source)
XLA Modules:
  0.0 1729.3 jit_solution(5218491819954297430)
XLA Ops:
  28.3 17.6 %all-to-all-done.1 = bf16[8,48,1792]{2,1,0:T(8,128)(2,1)S(1)} async-done(((bf16[8,48,1792]{2,1,0:T(8,128)(2,1)}), bf16[8,48,1792]{2,1,0:T(8,128)(2,1)S(1)}, u32[]{:S(2)}, u32[]{:S(2)}) %all-to-all-start.1) | async-done | bytes 1376288 | tf_op jit(solution)/shard_map/all_to_all | solution.py:183
  50.2 101.4 %all-gather.4.cloned.1.call-done = bf16[1536,1792]{1,0:T(8,128)(2,1)} async-done(((bf16[384,1792]{1,0:T(8,128)(2,1)}), bf16[1536,1792]{1,0:T(8,128)(2,1)}) %all-gather.4.cloned.1.call-update) | async-done | bytes 5505040 | tf_op jit(solution)/shard_map/all_gather | solution.py:213
  169.8 26.9 %while.30 = (s32[]{:T(128)}, bf16[3,512,4,112]{1,3,2,0:T(8,128)(2,1)}, f32[3,4,512]{2,1,0:T(4,128)S(1)}, s32[3]{0:T(128)S(1)}, bf16[1600,4,112]{0,2,1:T(8,128)(2...) while((s32[]{:T(128)}, ...), condition=%wide.region_12.13_spmd, body=%wide.region_9.12_spmd.sunk | while | flops 545521280 | bytes 17490852 | solution.py:81
  204.3 7.9 fusion.83
  216.9 23.1 %all_to_all.60 = bf16[8,48,1792]{2,1,0:T(8,128)(2,1)} all-to-all(bf16[8,48,1792]{2,1,0:T(8,128)(2,1)} %bitcast.130), channel_id=1, replica_groups=mesh['dp'=8,'mp'=4] {'dp'}, dimensions={0} | all-to-all | bytes 2752512 | tf_op jit(solution)/shard_map/all_to_all | solution.py:190
  244.7 341.4 %all-reduce.10.cloned.1.call-done = f32[1536,1792]{1,0:T(8,128)} async-done(((f32[1536,1792]{1,0:T(8,128)}), f32[1536,1792]{1,0:T(8,128)}) %all-reduce.10.cloned.1.call-update) | async-done | bytes 11010064 | tf_op jit(solution)/shard_map/psum | solution.py:227
  586.1 11.9 multiply_reduce_fusion.1
  603.1 11.6 fusion.84
  614.7 7.7 fusion.85
  622.4 66.7 %all-gather.6.cloned.1.call-done = bf16[1536,1792]{1,0:T(8,128)(2,1)} async-done(((bf16[384,1792]{1,0:T(8,128)(2,1)}), bf16[1536,1792]{1,0:T(8,128)(2,1)}) %all-gather.6.cloned.1.call-update) | async-done | bytes 5505040 | tf_op jit(solution)/shard_map/all_gather | solution.py:214
  689.1 16.0 multiply_convert_fusion.2
  705.1 8.5 fusion.86
  713.6 11.2 convolution_add_fusion
  726.9 182.8 %reduce-scatter.6.cloned.1.call-done = f32[384,1792]{1,0:T(8,128)} async-done(((f32[1536,1792]{1,0:T(8,128)}), f32[384,1792]{1,0:T(8,128)}) %reduce-scatter.6.cloned.1.call-update) | async-done | bytes 2752528 | tf_op jit(solution)/shard_map/reduce_scatter | solution.py:253
  918.3 103.5 %all-gather.8.cloned.1.call-done = bf16[1536,1792]{1,0:T(8,128)(2,1)} async-done(((bf16[384,1792]{1,0:T(8,128)(2,1)}), bf16[1536,1792]{1,0:T(8,128)(2,1)}) %all-gather.8.cloned.1.call-update) | async-done | bytes 5505040 | tf_op jit(solution)/shard_map/all_gather | solution.py:262
  1032.5 127.1 %while.31 = (s32[]{:T(128)}, f32[1600,4,112]{0,2,1:T(8,128)}, f32[1600,4,112]{0,2,1:T(8,128)}, bf16[3,512,4,112]{1,3,2,0:T(8,128)(2,1)}, s32[3]{0:T(128)S(1)}, /...) while((s32[]{:T(128)}, f32[1600,4,112]{0,2,1:T(8,128)}, ...), condition=%wide.region_24.25_spmd, body=%wide.region_22.24_spmd.sunk | while | flops 1342557824 | bytes 73204776 | solution.py:143
  1049.1 9.8 dynamic_update_slice.44
  1063.3 9.8 dynamic_update_slice.45
  1092.8 9.7 dynamic_update_slice.44
  1106.8 9.7 dynamic_update_slice.45
  1136.0 8.1 dynamic_update_slice.44
  1148.4 8.1 dynamic_update_slice.45
  1179.3 7.4 add_convert_fusion
  1186.9 10.1 convolution_convert_fusion
  1197.0 10.7 convolution_convert_fusion.1
  1207.8 10.3 convolution_convert_fusion.3
  1242.7 40.6 %reduce-scatter.8.cloned.1.call-done = bf16[384,1792]{1,0:T(8,128)(2,1)} async-done(((bf16[1536,1792]{1,0:T(8,128)(2,1)}), bf16[384,1792]{1,0:T(8,128)(2,1)}) %reduce-scatter.8.cloned.1.call-update) | async-done | bytes 1376272 | tf_op jit(solution)/shard_map/reduce_scatter | solution.py:279
  1285.6 99.1 %reduce-scatter.4.cloned.1.call-done = bf16[384,1792]{1,0:T(8,128)(2,1)} async-done(((bf16[1536,1792]{1,0:T(8,128)(2,1)}), bf16[384,1792]{1,0:T(8,128)(2,1)}) %reduce-scatter.4.cloned.1.call-update) | async-done | bytes 1376272 | tf_op jit(solution)/shard_map/reduce_scatter | solution.py:237
  1399.6 30.8 %all-to-all-done.2 = bf16[8,48,1792]{2,1,0:T(8,128)(2,1)S(1)} async-done(((bf16[8,48,1792]{2,1,0:T(8,128)(2,1)}), bf16[8,48,1792]{2,1,0:T(8,128)(2,1)S(1)}, u32[]{:S(2)}, u32[]{:S(2)}) %all-to-all-start.2) | async-done | bytes 1376288 | tf_op jit(solution)/shard_map/all_to_all | solution.py:302
  1435.0 213.3 %all-reduce.12.cloned.1.call-done = (bf16[1792,448]{0,1:T(8,128)(2,1)}, bf16[1792,448]{0,1:T(8,128)(2,1)}, bf16[1792,448]{0,1:T(8,128)(2,1)}, bf16[448,1792]{1,0...) async-done(((bf16[1792,448]{0,1:T(8,128)(2,1)}, bf16[1792,448]{0,1:T(8,128)(2,1)}, bf16[1792,448]{0,1:T(8,128)(2,1)}, ...) | async-done | bytes 17432592 | tf_op jit(solution)/shard_map/psum | solution.py:293
  1670.2 23.2 %all-reduce.4 = (f32[1792]{0:T(1024)S(1)}, f32[1792]{0:T(1024)S(1)}) all-reduce(f32[1792]{0:T(1024)S(1)} %get-tuple-element.307, f32[1792]{0:T(1024)S(1)} %copy-done.28), channel_id=1, replica_groups=mesh['dp'=8,'mp'=4] {'dp'}, use_global_device_ids=true, to_apply=%region_28.29 | all-reduce | flops 3584 | bytes 28672 | tf_op jit(solution)/shard_map/psum | solution.py:291
  1693.4 19.3 %all-reduce.5 = (f32[1792]{0:T(1024)}, f32[1792]{0:T(1024)}) all-reduce(f32[1792]{0:T(1024)S(1)} %get-tuple-element.355, f32[1792]{0:T(1024)S(1)} %get-tuple-element.356), channel_id=1, replica_groups=mesh['dp'=8,'mp'=4] {'mp'}, use_global_device_ids=true, to_apply=%region_29.30 | all-reduce | flops 3584 | bytes 28672 | tf_op jit(solution)/shard_map/psum | solution.py:291
  (300 shorter events, 278.3 us)
Async XLA Ops:
  7.2 197.1 %copy-start = (bf16[448,1792]{1,0:T(8,128)(2,1)S(1)}, bf16[448,1792]{1,0:T(8,128)(2,1)}, u32[]{:S(2)}) copy-start(bf16[448,1792]{1,0:T(8,128)(2,1)} %param.28) | copy-start | bytes 4816900
  9.3 203.0 %copy-start.31 = (s32[384]{0:T(512)}, s32[384]{0:T(512)S(1)}, u32[]{:S(2)}) copy-start(s32[384]{0:T(512)S(1)} %compare_select_fusion.1) | copy-start | bytes 4612
  12.9 9.8 all-to-all-start
  22.6 27.1 %copy-start.42 = (s32[1,3]{1,0:T(1,128)S(1)}, s32[1,3]{1,0:T(1,128)}, u32[]{:S(2)}) copy-start(s32[1,3]{1,0:T(1,128)} %param.21) | copy-start | bytes 40
  22.6 27.3 %copy-start.35 = (s32[1536]{0:T(1024)S(1)}, s32[1536]{0:T(1024)}, u32[]{:S(2)}) copy-start(s32[1536]{0:T(1024)} %param.22) | copy-start | bytes 18436
  22.6 23.2 %all-to-all-start.1 = ((bf16[8,48,1792]{2,1,0:T(8,128)(2,1)}), bf16[8,48,1792]{2,1,0:T(8,128)(2,1)S(1)}, u32[]{:S(2)}, u32[]{:S(2)}) async-start(bf16[8,48,1792]{2,1,0:T(8,128)(2,1)} %bitcast.14), calls=%async_computation.1 | async-start | bytes 2752512 | tf_op jit(solution)/shard_map/all_to_all | solution.py:183
  26.9 124.7 %all-gather.4.cloned.1.call-start = ((), (), s32[]{:S(2)}) async-start(), calls=%async_computation.8 | async-start | bytes 6881280 | tf_op jit(solution)/shard_map/all_gather | solution.py:213
  28.3 211.7 %copy-start.33 = (s32[384]{0:T(512)}, s32[384]{0:T(512)S(1)}, u32[]{:S(2)}) copy-start(s32[384]{0:T(512)S(1)} %fusion.79) | copy-start | bytes 4612
  49.7 536.4 %all-reduce.10.cloned.1.call-start = ((), (), s32[]{:S(2)}) async-start(), calls=%async_computation.9 | async-start | bytes 22020096 | tf_op jit(solution)/shard_map/psum | solution.py:227
  50.2 105.3 %copy-start.24 = (f32[1792]{0:T(1024)S(1)}, f32[1792]{0:T(1024)}, u32[]{:S(2)}) copy-start(f32[1792]{0:T(1024)} %param.23) | copy-start | bytes 21508
  212.2 476.8 %all-gather.6.cloned.1.call-start = ((), (), s32[]{:S(2)}) async-start(), calls=%async_computation.11 | async-start | bytes 6881280 | tf_op jit(solution)/shard_map/all_gather | solution.py:214
  244.6 353.4 %copy-start.22 = (f32[1792]{0:T(1024)S(1)}, f32[1792]{0:T(1024)}, u32[]{:S(2)}) copy-start(f32[1792]{0:T(1024)} %param.24) | copy-start | bytes 21508
  244.6 665.2 %reduce-scatter.6.cloned.1.call-start = ((), (), s32[]{:S(2)}) async-start(), calls=%async_computation.12 | async-start | bytes 13762560 | tf_op jit(solution)/shard_map/reduce_scatter | solution.py:253
  603.1 11.6 copy-start.7
  603.1 11.6 copy-start.37
  689.1 16.0 copy-start.36
  724.8 297.0 %all-gather.8.cloned.1.call-start = ((), (), s32[]{:S(2)}) async-start(), calls=%async_computation.13 | async-start | bytes 6881280 | tf_op jit(solution)/shard_map/all_gather | solution.py:262
  726.9 186.9 %copy-start.26 = (f32[384]{0:T(512)}, f32[384]{0:T(512)S(1)}, u32[]{:S(2)}) copy-start(f32[384]{0:T(512)S(1)} %add_rsqrt_fusion.3) | copy-start | bytes 4612
  918.2 365.1 %reduce-scatter.8.cloned.1.call-start = ((), (), s32[]{:S(2)}) async-start(), calls=%async_computation.14 | async-start | bytes 6881280 | tf_op jit(solution)/shard_map/reduce_scatter | solution.py:279
  1186.8 197.9 %reduce-scatter.4.cloned.1.call-start = ((), (), s32[]{:S(2)}) async-start(), calls=%async_computation.10 | async-start | bytes 6881280 | tf_op jit(solution)/shard_map/reduce_scatter | solution.py:237
  1197.0 451.2 %all-reduce.12.cloned.1.call-start = ((), (), s32[]{:S(2)}) async-start(), calls=%async_computation.15 | async-start | bytes 34865152 | tf_op jit(solution)/shard_map/psum | solution.py:293
  1197.0 10.8 copy-start.46
  1197.0 21.1 %slice-start.2 = ((s8[5505024]{0:T(1024)(128)(4,1)}), s8[4194304]{0:T(1024)(128)(4,1)S(1)}, s32[]{:S(2)}) async-start(s8[5505024]{0:T(1024)(128)(4,1)} %bitcast.124), calls=%async_computation.18 | async-start | bytes 8388608
  1207.8 17.8 %slice-start.4 = ((s8[5505024]{0:T(1024)(128)(4,1)}), s8[4194304]{0:T(1024)(128)(4,1)S(1)}, s32[]{:S(2)}) async-start(s8[5505024]{0:T(1024)(128)(4,1)} %bitcast.128), calls=%async_computation.20 | async-start | bytes 8388608
  1225.6 11.6 slice-start.6
  1241.0 42.3 %copy-start.25 = (f32[1792]{0:T(1024)S(1)}, f32[1792]{0:T(1024)}, u32[]{:S(2)}) copy-start(f32[1792]{0:T(1024)} %param.23) | copy-start | bytes 21508
  1241.7 143.1 %copy-start.23 = (f32[1792]{0:T(1024)S(1)}, f32[1792]{0:T(1024)}, u32[]{:S(2)}) copy-start(f32[1792]{0:T(1024)} %param.24) | copy-start | bytes 21508
  1241.7 143.1 %copy-start.27 = (f32[384]{0:T(512)S(1)}, f32[384]{0:T(512)}, u32[]{:S(2)}) copy-start(f32[384]{0:T(512)} %copy-done.26) | copy-start | bytes 4612
  1241.7 143.1 %copy-start.30 = (f32[384]{0:T(512)S(1)}, f32[384]{0:T(512)}, u32[]{:S(2)}) copy-start(f32[384]{0:T(512)} %copy-done.29) | copy-start | bytes 4612
  1392.9 37.5 %all-to-all-start.2 = ((bf16[8,48,1792]{2,1,0:T(8,128)(2,1)}), bf16[8,48,1792]{2,1,0:T(8,128)(2,1)S(1)}, u32[]{:S(2)}, u32[]{:S(2)}) async-start(bf16[8,48,1792]{2,1,0:T(8,128)(2,1)} %bitcast.127), calls=%async_computation.3 | async-start | bytes 2752512 | tf_op jit(solution)/shard_map/all_to_all | solution.py:302
  1399.6 35.4 %copy-start.32 = (s32[384]{0:T(512)S(1)}, s32[384]{0:T(512)}, u32[]{:S(2)}) copy-start(s32[384]{0:T(512)} %copy-done.31) | copy-start | bytes 4612
  1430.4 285.4 %all-to-all-start.4 = ((bf16[8,48,1792]{2,1,0:T(8,128)(2,1)}), bf16[8,48,1792]{2,1,0:T(8,128)(2,1)}, u32[]{:S(2)}, u32[]{:S(2)}) async-start(bf16[8,48,1792]{2,1,0:T(8,128)(2,1)} %bitcast.126), calls=%async_computation.7 | async-start | bytes 2752512 | tf_op jit(solution)/shard_map/all_to_all | solution.py:309
  (41 other events, 183.7 us)
Sparse Core Ops, SparseCore 0:
  49.8 101.7 all-gather.3
  212.3 373.7 all-reduce.9
  587.7 101.3 all-gather.5
  724.9 184.7 reduce-scatter.5
  918.3 103.4 all-gather.7
  1186.9 96.3 reduce-scatter.7
  1286.2 98.5 reduce-scatter.3
  1390.5 257.6 all-reduce.11
